TPU v7x, 512 devices: a whole 4x4x16 slice. The times are simulated.
512 devices in a mesh: fsdp: 16 (over z), replica: 16 (over x_lo, y, core), tm: 2 (over x_hi).
Axes of the slice: x: 4 (x_hi: 2, x_lo: 2; x = x_hi * 2 + x_lo), y: 4, z: 16, core: 2. Of those that a mesh axis runs over, the one named last changes fastest.
Arguments:
- clip_input: bfloat16 [16, 8, 16, 16, 512], P('replica', 'tm'), may hold values from -6 to 6
- first_kernel: bfloat16 [27, 512, 512], P(None, None, 'fsdp'), may hold values from -0.0546875 to 0.0546875
- second_kernel: bfloat16 [27, 512, 512], P(None, 'fsdp'), may hold values from -0.0546875 to 0.0546875
- out_grad: bfloat16 [16, 2, 4, 4, 512], P('replica', 'tm'), may hold values from -1 to 1
- tap_mix: float32 [2, 27, 27], replicated, may hold values from -0.14 to 1.4
- left_panels: float32 [2, 512, 512], P(None, 'fsdp'), may hold values from -0.05 to 2
- right_panels: float32 [2, 512, 512], P(None, 'fsdp', ('replica', 'tm')), may hold values from -0.05 to 2
Outputs:
- update: bfloat16 [2, 27, 512, 512], P(None, None, 'fsdp', ('replica', 'tm'))
All inputs are finite; a program needn't handle non-finite values.
Results may differ from a plain program's by a relative error of at most 0.0049.
Values may be sent and summed in bfloat16 or wider, within the bound.
A program may use at most 128 MiB of HBM per device.

v0:
```python
import jax
import jax.numpy as jnp
from jax import lax
from jax.sharding import PartitionSpec as P

TAPS = 27


def shifted(block, axis, distance):
    devices = range(lax.axis_size(axis))
    route = [(i - distance, i) for i in devices if i - distance in devices]
    return lax.ppermute(block, axis, route)


def tap_patches(padded, out_frames, out_side):
    pieces_list = []
    for tap_index in range(TAPS):
        along_time = tap_index // 9
        along_rows = tap_index // 3 % 3
        along_cols = tap_index % 3
        pieces_list.append(
            padded[
                :,
                along_time : along_time + 2 * out_frames : 2,
                along_rows : along_rows + 2 * out_side : 2,
                along_cols : along_cols + 2 * out_side : 2,
                :,
            ]
        )
    return jnp.concatenate(pieces_list, axis=-1)


def spread_back(grad_shape, columns, out_frames, out_side, channels):
    total = jnp.zeros(grad_shape, jnp.float32)
    for tap_index in range(TAPS):
        along_time = tap_index // 9
        along_rows = tap_index // 3 % 3
        along_cols = tap_index % 3
        total = total.at[
            :,
            along_time : along_time + 2 * out_frames : 2,
            along_rows : along_rows + 2 * out_side : 2,
            along_cols : along_cols + 2 * out_side : 2,
            :,
        ].add(columns[..., tap_index * channels : (tap_index + 1) * channels])
    return total


def shards(clip_input, first_kernel, second_kernel, out_grad, tap_mix, left_panels, right_panels):
    highest = lax.Precision.HIGHEST
    clip_count = clip_input.shape[0]
    frames = clip_input.shape[1]
    side_cells = clip_input.shape[2]
    channels = clip_input.shape[4]
    own_width = first_kernel.shape[2]
    half_frames = frames // 2
    half_side = side_cells // 2
    quarter_frames = frames // 4
    quarter_side = side_cells // 4
    spatial_pad = ((0, 0), (0, 0), (1, 0), (1, 0), (0, 0))
    flat_kernel = first_kernel.reshape(TAPS * channels, own_width)
    prior_frame = shifted(clip_input[:, frames - 1 :], "tm", 1)
    extended = jnp.concatenate([prior_frame, clip_input], axis=1)
    padded_input = jnp.pad(extended, spatial_pad)
    first_patches = tap_patches(padded_input, half_frames, half_side).reshape(-1, TAPS * channels)
    pre_act = jnp.dot(first_patches, flat_kernel, preferred_element_type=jnp.float32)
    hidden = (
        jax.nn.silu(pre_act)
        .astype(jnp.bfloat16)
        .reshape(clip_count, half_frames, half_side, half_side, own_width)
    )
    prior_hidden = shifted(hidden[:, half_frames - 1 :], "tm", 1)
    padded_hidden = jnp.pad(jnp.concatenate([prior_hidden, hidden], axis=1), spatial_pad)
    second_patches = tap_patches(padded_hidden, quarter_frames, quarter_side).reshape(
        -1, TAPS * own_width
    )
    grad_rows = out_grad.reshape(-1, channels)
    second_grad = jnp.dot(grad_rows.T, second_patches, preferred_element_type=jnp.float32)
    second_grad = second_grad.reshape(channels, TAPS, own_width).transpose(1, 0, 2)
    back_columns = jnp.dot(
        grad_rows,
        second_kernel.reshape(TAPS * own_width, channels).T,
        preferred_element_type=jnp.float32,
    )
    back_columns = back_columns.reshape(
        clip_count, quarter_frames, quarter_side, quarter_side, TAPS * own_width
    )
    spread = spread_back(padded_hidden.shape, back_columns, quarter_frames, quarter_side, own_width)
    returned = shifted(spread[:, :1, 1:, 1:, :], "tm", -1)
    hidden_grad = spread[:, 1:, 1:, 1:, :]
    hidden_grad = hidden_grad.at[:, half_frames - 1 :].add(returned).reshape(-1, own_width)
    sigmoid_vals = jax.nn.sigmoid(pre_act)
    pre_grad = (hidden_grad * sigmoid_vals * (1.0 + pre_act * (1.0 - sigmoid_vals))).astype(
        jnp.bfloat16
    )
    first_grad = jnp.dot(first_patches.T, pre_grad, preferred_element_type=jnp.float32).reshape(
        TAPS, channels, own_width
    )
    stacked = jnp.stack([first_grad, second_grad])
    summed = lax.psum(stacked, ("replica", "tm"))
    tap_mixed = jnp.einsum("lst,ltij->lsij", tap_mix, summed, precision=highest)
    left_done = jnp.einsum(
        "lik,lskj->lsij",
        lax.all_gather(left_panels, "fsdp", axis=1, tiled=True),
        tap_mixed,
        precision=highest,
    )
    result = lax.psum_scatter(
        jnp.einsum("lsij,ljk->ilsk", left_done, right_panels, precision=highest),
        "fsdp",
        scatter_dimension=0,
        tiled=True,
    ).transpose(1, 2, 0, 3)
    return result.astype(jnp.bfloat16)


def solution(mesh):
    in_specs = (
        P("replica", "tm", None, None, None),
        P(None, None, "fsdp"),
        P(None, "fsdp", None),
        P("replica", "tm", None, None, None),
        P(),
        P(None, "fsdp", None),
        P(None, "fsdp", ("replica", "tm")),
    )
    out_specs = P(None, None, "fsdp", ("replica", "tm"))
    return jax.shard_map(shards, mesh=mesh, in_specs=in_specs, out_specs=out_specs, check_vma=False)
```

profile of v0, /device:TPU:4, one launch (start us, length us, event | category | flops | bytes accessed | tf_op | source)
XLA Modules:
  0.0 490.1 jit_solution(18250001880252223688)
XLA Ops:
  55.4 7.8 %collective-permute-start.1 = (f32[1,1,8,8,32]{4,1,3,2,0:T(1,128)S(1)}, f32[1,1,8,8,32]{4,1,3,2,0:T(1,128)S(1)}, u32[]{:S(2)}, u32[]{:S(2)}) collective-permute-start(f32[1,1,8,8,32]{4,1,3,2,0:T(1,128)S(1)} %slice.702), channel_id=1, source_target_pairs={{1,0},{3,2},{5,4},{7,6},{9,8},{11,10},{13,12},{15,14},{17,16},{19,... | collective-permute-start | bytes 24584 | tf_op jit(solution)/shard_map/ppermute | solution.py:12
  67.2 5.0 %slice.318 = bf16[1,2,8,8,512]{4,3,2,1,0:T(8,128)(2,1)} slice(bf16[1,5,17,17,512]{4,3,2,1,0:T(8,128)(2,1)S(1)} %fusion.15), slice={[0:1:1], [0:4:2], [0:16:2], [0:16:2], [0:512:1]} | slice | bytes 262144 | tf_op jit(solution)/shard_map/slice | solution.py:22
  72.2 4.9 %slice.319 = bf16[1,2,8,8,512]{4,3,2,1,0:T(8,128)(2,1)} slice(bf16[1,5,17,17,512]{4,3,2,1,0:T(8,128)(2,1)S(1)} %fusion.15), slice={[0:1:1], [0:4:2], [0:16:2], [1:17:2], [0:512:1]} | slice | bytes 262144 | tf_op jit(solution)/shard_map/slice | solution.py:22
  77.1 5.0 %slice.320 = bf16[1,2,8,8,512]{4,3,2,1,0:T(8,128)(2,1)} slice(bf16[1,5,17,17,512]{4,3,2,1,0:T(8,128)(2,1)S(1)} %fusion.15), slice={[0:1:1], [0:4:2], [0:16:2], [2:17:2], [0:512:1]} | slice | bytes 262144 | tf_op jit(solution)/shard_map/slice | solution.py:22
  82.1 4.9 %slice.321 = bf16[1,2,8,8,512]{4,3,2,1,0:T(8,128)(2,1)} slice(bf16[1,5,17,17,512]{4,3,2,1,0:T(8,128)(2,1)S(1)} %fusion.15), slice={[0:1:1], [0:4:2], [1:17:2], [0:16:2], [0:512:1]} | slice | bytes 262144 | tf_op jit(solution)/shard_map/slice | solution.py:22
  87.0 4.9 %slice.322 = bf16[1,2,8,8,512]{4,3,2,1,0:T(8,128)(2,1)} slice(bf16[1,5,17,17,512]{4,3,2,1,0:T(8,128)(2,1)S(1)} %fusion.15), slice={[0:1:1], [0:4:2], [1:17:2], [1:17:2], [0:512:1]} | slice | bytes 262144 | tf_op jit(solution)/shard_map/slice | solution.py:22
  91.9 5.0 %slice.323 = bf16[1,2,8,8,512]{4,3,2,1,0:T(8,128)(2,1)} slice(bf16[1,5,17,17,512]{4,3,2,1,0:T(8,128)(2,1)S(1)} %fusion.15), slice={[0:1:1], [0:4:2], [1:17:2], [2:17:2], [0:512:1]} | slice | bytes 262144 | tf_op jit(solution)/shard_map/slice | solution.py:22
  96.9 5.0 %slice.324 = bf16[1,2,8,8,512]{4,3,2,1,0:T(8,128)(2,1)} slice(bf16[1,5,17,17,512]{4,3,2,1,0:T(8,128)(2,1)S(1)} %fusion.15), slice={[0:1:1], [0:4:2], [2:17:2], [0:16:2], [0:512:1]} | slice | bytes 262144 | tf_op jit(solution)/shard_map/slice | solution.py:22
  101.9 4.9 %slice.325 = bf16[1,2,8,8,512]{4,3,2,1,0:T(8,128)(2,1)} slice(bf16[1,5,17,17,512]{4,3,2,1,0:T(8,128)(2,1)S(1)} %fusion.15), slice={[0:1:1], [0:4:2], [2:17:2], [1:17:2], [0:512:1]} | slice | bytes 262144 | tf_op jit(solution)/shard_map/slice | solution.py:22
  106.8 5.0 %slice.326 = bf16[1,2,8,8,512]{4,3,2,1,0:T(8,128)(2,1)} slice(bf16[1,5,17,17,512]{4,3,2,1,0:T(8,128)(2,1)S(1)} %fusion.15), slice={[0:1:1], [0:4:2], [2:17:2], [2:17:2], [0:512:1]} | slice | bytes 262144 | tf_op jit(solution)/shard_map/slice | solution.py:22
  111.8 4.9 %slice.327 = bf16[1,2,8,8,512]{4,3,2,1,0:T(8,128)(2,1)} slice(bf16[1,5,17,17,512]{4,3,2,1,0:T(8,128)(2,1)S(1)} %fusion.15), slice={[0:1:1], [1:5:2], [0:16:2], [0:16:2], [0:512:1]} | slice | bytes 262144 | tf_op jit(solution)/shard_map/slice | solution.py:22
  116.7 4.9 %slice.328 = bf16[1,2,8,8,512]{4,3,2,1,0:T(8,128)(2,1)} slice(bf16[1,5,17,17,512]{4,3,2,1,0:T(8,128)(2,1)S(1)} %fusion.15), slice={[0:1:1], [1:5:2], [0:16:2], [1:17:2], [0:512:1]} | slice | bytes 262144 | tf_op jit(solution)/shard_map/slice | solution.py:22
  121.7 5.0 %slice.329 = bf16[1,2,8,8,512]{4,3,2,1,0:T(8,128)(2,1)} slice(bf16[1,5,17,17,512]{4,3,2,1,0:T(8,128)(2,1)S(1)} %fusion.15), slice={[0:1:1], [1:5:2], [0:16:2], [2:17:2], [0:512:1]} | slice | bytes 262144 | tf_op jit(solution)/shard_map/slice | solution.py:22
  126.6 4.9 %slice.330 = bf16[1,2,8,8,512]{4,3,2,1,0:T(8,128)(2,1)} slice(bf16[1,5,17,17,512]{4,3,2,1,0:T(8,128)(2,1)S(1)} %fusion.15), slice={[0:1:1], [1:5:2], [1:17:2], [0:16:2], [0:512:1]} | slice | bytes 262144 | tf_op jit(solution)/shard_map/slice | solution.py:22
  131.5 4.9 %slice.331 = bf16[1,2,8,8,512]{4,3,2,1,0:T(8,128)(2,1)} slice(bf16[1,5,17,17,512]{4,3,2,1,0:T(8,128)(2,1)S(1)} %fusion.15), slice={[0:1:1], [1:5:2], [1:17:2], [1:17:2], [0:512:1]} | slice | bytes 262144 | tf_op jit(solution)/shard_map/slice | solution.py:22
  136.5 5.0 %slice.332 = bf16[1,2,8,8,512]{4,3,2,1,0:T(8,128)(2,1)} slice(bf16[1,5,17,17,512]{4,3,2,1,0:T(8,128)(2,1)S(1)} %fusion.15), slice={[0:1:1], [1:5:2], [1:17:2], [2:17:2], [0:512:1]} | slice | bytes 262144 | tf_op jit(solution)/shard_map/slice | solution.py:22
  141.4 4.9 %slice.333 = bf16[1,2,8,8,512]{4,3,2,1,0:T(8,128)(2,1)} slice(bf16[1,5,17,17,512]{4,3,2,1,0:T(8,128)(2,1)S(1)} %fusion.15), slice={[0:1:1], [1:5:2], [2:17:2], [0:16:2], [0:512:1]} | slice | bytes 262144 | tf_op jit(solution)/shard_map/slice | solution.py:22
  146.4 4.9 %slice.334 = bf16[1,2,8,8,512]{4,3,2,1,0:T(8,128)(2,1)} slice(bf16[1,5,17,17,512]{4,3,2,1,0:T(8,128)(2,1)S(1)} %fusion.15), slice={[0:1:1], [1:5:2], [2:17:2], [1:17:2], [0:512:1]} | slice | bytes 262144 | tf_op jit(solution)/shard_map/slice | solution.py:22
  151.3 5.0 %slice.335 = bf16[1,2,8,8,512]{4,3,2,1,0:T(8,128)(2,1)} slice(bf16[1,5,17,17,512]{4,3,2,1,0:T(8,128)(2,1)S(1)} %fusion.15), slice={[0:1:1], [1:5:2], [2:17:2], [2:17:2], [0:512:1]} | slice | bytes 262144 | tf_op jit(solution)/shard_map/slice | solution.py:22
  156.3 4.9 %slice.336 = bf16[1,2,8,8,512]{4,3,2,1,0:T(8,128)(2,1)} slice(bf16[1,5,17,17,512]{4,3,2,1,0:T(8,128)(2,1)S(1)} %fusion.15), slice={[0:1:1], [2:5:2], [0:16:2], [0:16:2], [0:512:1]} | slice | bytes 262144 | tf_op jit(solution)/shard_map/slice | solution.py:22
  161.2 4.9 %slice.337 = bf16[1,2,8,8,512]{4,3,2,1,0:T(8,128)(2,1)} slice(bf16[1,5,17,17,512]{4,3,2,1,0:T(8,128)(2,1)S(1)} %fusion.15), slice={[0:1:1], [2:5:2], [0:16:2], [1:17:2], [0:512:1]} | slice | bytes 262144 | tf_op jit(solution)/shard_map/slice | solution.py:22
  166.1 5.0 %slice.338 = bf16[1,2,8,8,512]{4,3,2,1,0:T(8,128)(2,1)} slice(bf16[1,5,17,17,512]{4,3,2,1,0:T(8,128)(2,1)S(1)} %fusion.15), slice={[0:1:1], [2:5:2], [0:16:2], [2:17:2], [0:512:1]} | slice | bytes 262144 | tf_op jit(solution)/shard_map/slice | solution.py:22
  171.1 4.9 %slice.339 = bf16[1,2,8,8,512]{4,3,2,1,0:T(8,128)(2,1)} slice(bf16[1,5,17,17,512]{4,3,2,1,0:T(8,128)(2,1)S(1)} %fusion.15), slice={[0:1:1], [2:5:2], [1:17:2], [0:16:2], [0:512:1]} | slice | bytes 262144 | tf_op jit(solution)/shard_map/slice | solution.py:22
  176.0 4.9 %slice.340 = bf16[1,2,8,8,512]{4,3,2,1,0:T(8,128)(2,1)} slice(bf16[1,5,17,17,512]{4,3,2,1,0:T(8,128)(2,1)S(1)} %fusion.15), slice={[0:1:1], [2:5:2], [1:17:2], [1:17:2], [0:512:1]} | slice | bytes 262144 | tf_op jit(solution)/shard_map/slice | solution.py:22
  214.9 6.0 %copy.17 = bf16[128,13824]{0,1:T(8,128)(2,1)} copy(bf16[128,13824]{1,0:T(8,128)(2,1)} %bitcast) | data formatting | bytes 7077888 | tf_op jit(solution)/shard_map/reshape | solution.py:65
  220.9 3.2 multiply_convert_fusion
  225.6 3.3 convolution_bitcast_fusion
  228.9 2.5 collective-permute-done.2
  239.2 143.1 %all-reduce.4.cloned.1.call-done = f32[2,27,512,32]{2,3,1,0:T(8,128)} async-done(((f32[2,27,512,32]{2,3,1,0:T(8,128)}), f32[2,27,512,32]{2,3,1,0:T(8,128)}) %all-reduce.4.cloned.1.call-update) | async-done | bytes 3538960 | tf_op jit(solution)/shard_map/psum | solution.py:100
  382.2 10.7 %fusion.11 = f32[2,27,512,32]{2,1,3,0:T(8,128)} fusion(f32[2,27,512,32]{2,3,1,0:T(8,128)} %all-reduce.4.cloned.1.call-done, f32[2,27,27,1]{2,0,1,3:T(2,128)S(1)} %bitcast.215), kind=kOutput, calls=%fused_computation.41 | convolution fusion | flops 286654464 | bytes 7083720 | tf_op jit(solution)/shard_map/lst,ltij->lsij/dot_general | solution.py:101
  393.0 10.1 %fusion.7 = f32[2,27,32,512]{3,2,1,0:T(8,128)S(1)} fusion(f32[2,27,512,32]{2,1,3,0:T(8,128)} %fusion.11, f32[2,512,512]{2,1,0:T(8,128)} %all-gather.2.cloned.1.call-done), kind=kOutput, calls=%fused_computation.37 | convolution fusion | flops 5435817984 | bytes 9175040 | tf_op jit(solution)/shard_map/lik,lskj->lsij/dot_general | solution.py:102
  406.9 73.8 %reduce-scatter.4.cloned.1.call-done = f32[32,864]{1,0:T(8,128)} async-done(((f32[512,864]{1,0:T(8,128)}), f32[32,864]{1,0:T(8,128)}) %reduce-scatter.4.cloned.1.call-update) | async-done | bytes 110608
  (206 shorter events, 99.8 us)
Async XLA Ops:
  7.4 3.1 copy-start
  7.4 55.8 %copy-start.2 = (bf16[27,512,32]{1,2,0:T(8,128)(2,1)S(1)}, bf16[27,512,32]{1,2,0:T(8,128)(2,1)}, u32[]{:S(2)}) copy-start(bf16[27,512,32]{1,2,0:T(8,128)(2,1)} %param.10) | copy-start | bytes 2654212
  7.4 374.9 %all-reduce.4.cloned.1.call-start = ((), (), s32[]{:S(2)}) async-start(), calls=%async_computation.1 | async-start | bytes 7077888 | tf_op jit(solution)/shard_map/psum | solution.py:100
  8.5 56.6 %collective-permute-start = (bf16[1,1,16,16,512]{4,3,2,1,0:T(8,128)(2,1)S(1)}, bf16[1,1,16,16,512]{4,3,2,1,0:T(8,128)(2,1)S(1)}, u32[]{:S(2)}, u32[]{:S(2)}) collective-permute-start(bf16[1,1,16,16,512]{4,3,2,1,0:T(8,128)(2,1)S(1)} %slice.317), channel_id=1, source_target_pairs={{0,1},{2,3},{4,5},{6,7},{8,9},{10,11},{12,13},{14,15},{16,17},{18,... | collective-permute-start | bytes 786440 | tf_op jit(solution)/shard_map/ppermute | solution.py:12
  55.4 9.4 %collective-permute-start.1 = (f32[1,1,8,8,32]{4,1,3,2,0:T(1,128)S(1)}, f32[1,1,8,8,32]{4,1,3,2,0:T(1,128)S(1)}, u32[]{:S(2)}, u32[]{:S(2)}) collective-permute-start(f32[1,1,8,8,32]{4,1,3,2,0:T(1,128)S(1)} %slice.702), channel_id=1, source_target_pairs={{1,0},{3,2},{5,4},{7,6},{9,8},{11,10},{13,12},{15,14},{17,16},{19,... | collective-permute-start | bytes 24584 | tf_op jit(solution)/shard_map/ppermute | solution.py:12
  183.7 22.4 %copy-start.11 = (bf16[1,2,8,8,512]{4,3,2,1,0:T(8,128)(2,1)S(1)}, bf16[1,2,8,8,512]{4,3,2,1,0:T(8,128)(2,1)}, u32[]{:S(2)}) copy-start(bf16[1,2,8,8,512]{4,3,2,1,0:T(8,128)(2,1)} %slice.332) | copy-start | bytes 393220
  183.7 23.1 %copy-start.10 = (bf16[1,2,8,8,512]{4,3,2,1,0:T(8,128)(2,1)S(1)}, bf16[1,2,8,8,512]{4,3,2,1,0:T(8,128)(2,1)}, u32[]{:S(2)}) copy-start(bf16[1,2,8,8,512]{4,3,2,1,0:T(8,128)(2,1)} %slice.333) | copy-start | bytes 393220
  183.7 23.7 %copy-start.9 = (bf16[1,2,8,8,512]{4,3,2,1,0:T(8,128)(2,1)S(1)}, bf16[1,2,8,8,512]{4,3,2,1,0:T(8,128)(2,1)}, u32[]{:S(2)}) copy-start(bf16[1,2,8,8,512]{4,3,2,1,0:T(8,128)(2,1)} %slice.334) | copy-start | bytes 393220
  183.7 24.4 %copy-start.8 = (bf16[1,2,8,8,512]{4,3,2,1,0:T(8,128)(2,1)S(1)}, bf16[1,2,8,8,512]{4,3,2,1,0:T(8,128)(2,1)}, u32[]{:S(2)}) copy-start(bf16[1,2,8,8,512]{4,3,2,1,0:T(8,128)(2,1)} %slice.335) | copy-start | bytes 393220
  183.7 25.1 %copy-start.7 = (bf16[1,2,8,8,512]{4,3,2,1,0:T(8,128)(2,1)S(1)}, bf16[1,2,8,8,512]{4,3,2,1,0:T(8,128)(2,1)}, u32[]{:S(2)}) copy-start(bf16[1,2,8,8,512]{4,3,2,1,0:T(8,128)(2,1)} %slice.336) | copy-start | bytes 393220
  183.7 25.8 %copy-start.6 = (bf16[1,2,8,8,512]{4,3,2,1,0:T(8,128)(2,1)S(1)}, bf16[1,2,8,8,512]{4,3,2,1,0:T(8,128)(2,1)}, u32[]{:S(2)}) copy-start(bf16[1,2,8,8,512]{4,3,2,1,0:T(8,128)(2,1)} %slice.337) | copy-start | bytes 393220
  183.7 26.4 %copy-start.5 = (bf16[1,2,8,8,512]{4,3,2,1,0:T(8,128)(2,1)S(1)}, bf16[1,2,8,8,512]{4,3,2,1,0:T(8,128)(2,1)}, u32[]{:S(2)}) copy-start(bf16[1,2,8,8,512]{4,3,2,1,0:T(8,128)(2,1)} %slice.338) | copy-start | bytes 393220
  183.7 27.1 %copy-start.4 = (bf16[1,2,8,8,512]{4,3,2,1,0:T(8,128)(2,1)S(1)}, bf16[1,2,8,8,512]{4,3,2,1,0:T(8,128)(2,1)}, u32[]{:S(2)}) copy-start(bf16[1,2,8,8,512]{4,3,2,1,0:T(8,128)(2,1)} %slice.339) | copy-start | bytes 393220
  183.7 27.7 %copy-start.3 = (bf16[1,2,8,8,512]{4,3,2,1,0:T(8,128)(2,1)S(1)}, bf16[1,2,8,8,512]{4,3,2,1,0:T(8,128)(2,1)}, u32[]{:S(2)}) copy-start(bf16[1,2,8,8,512]{4,3,2,1,0:T(8,128)(2,1)} %slice.340) | copy-start | bytes 393220
  214.9 6.0 %copy-start.1 = (bf16[27,4,8,512]{3,2,0,1:T(8,128)(2,1)S(1)}, bf16[27,4,8,512]{3,2,0,1:T(8,128)(2,1)}, u32[]{:S(2)}) copy-start(bf16[27,4,8,512]{3,2,0,1:T(8,128)(2,1)} %copy.34) | copy-start | bytes 2654212
  224.1 11.5 %copy-start.14 = (bf16[1,1,4,4,512]{4,3,2,1,0:T(4,128)(2,1)S(1)}, bf16[1,1,4,4,512]{4,3,2,1,0:T(4,128)(2,1)}, u32[]{:S(2)}) copy-start(bf16[1,1,4,4,512]{4,3,2,1,0:T(4,128)(2,1)} %param.12) | copy-start | bytes 49156
  224.3 7.1 %collective-permute-start.2 = (bf16[1,1,8,8,32]{4,3,2,1,0:T(8,128)(2,1)S(1)}, bf16[1,1,8,8,32]{4,3,2,1,0:T(8,128)(2,1)S(1)}, u32[]{:S(2)}, u32[]{:S(2)}) collective-permute-start(bf16[1,1,8,8,32]{4,3,2,1,0:T(8,128)(2,1)S(1)} %slice.703), channel_id=1, source_target_pairs={{0,1},{2,3},{4,5},{6,7},{8,9},{10,11},{12,13},{14,15},{16,17},{18,... | collective-permute-start | bytes 12296 | tf_op jit(solution)/shard_map/ppermute | solution.py:12
  238.3 143.9 %copy-start.12 = (f32[2,27,27]{2,0,1:T(2,128)S(1)}, f32[2,27,27]{2,0,1:T(2,128)}, u32[]{:S(2)}) copy-start(f32[2,27,27]{2,0,1:T(2,128)} %param.13) | copy-start | bytes 17500
  238.3 154.6 %all-gather.2.cloned.1.call-start = ((), (), s32[]{:S(2)}) async-start(), calls=%async_computation.2 | async-start | bytes 2228224 | tf_op jit(solution)/shard_map/all_gather | solution.py:104
  238.9 241.7 %reduce-scatter.4.cloned.1.call-start = ((), (), s32[]{:S(2)}) async-start(), calls=%async_computation.3 | async-start | bytes 1949696
  393.0 10.1 %copy-start.13 = (f32[2,32,16]{1,2,0:T(8,128)S(1)}, f32[2,32,16]{1,2,0:T(8,128)}, u32[]{:S(2)}) copy-start(f32[2,32,16]{1,2,0:T(8,128)} %param.15) | copy-start | bytes 12292
Sparse Core Ops, SparseCore 0:
  238.5 143.7 all-reduce.3
Sparse Core Ops, SparseCore 1:
  240.9 75.5 all-gather.1
  406.9 73.6 reduce-scatter.3
where the time goes:
time: 500 us; the launch traced here: 490 us
  waiting for transfers between devices  220 us (44%)
  local copies, waits for them, and re-layouts  166 us (33%)
  other arithmetic  45.8 us (9%)
  matrix products  30.9 us (6%)
  between operations  16 us (3%)
  starting transfers between devices  10.7 us (2%)
    psum x1, waiting for transfers between devices, shards(): summed = lax.psum(stacked, ('replica', 'tm'))  143 us
    slice x54, local copies, waits for them, and re-layouts, tap_patches(): padded[:, along_time:along_time + 2 * out_frames:2, along_rows:along_rows...  120 us
    unnamed x4, waiting for transfers between devices  74.3 us
    scatter-add x27, other arithmetic, spread_back(): total = total.at[:, along_time:along_time + 2 * out_frames:2, along_rows:...  40.8 us
    unnamed x58, local copies, waits for them, and re-layouts  33.9 us
    dot_general x1, matrix products, shards(): tap_mixed = jnp.einsum('lst,ltij->lsij', tap_mix, summed, precision=highest)  10.7 us
    ppermute x3, starting transfers between devices, shifted(): return lax.ppermute(block, axis, route)  10.4 us
    dot_general x1, matrix products, shards(): jnp.einsum('lik,lskj->lsij', lax.all_gather(left_panels, 'fsdp', axis=1,...  10.1 us
  transfers between devices with their start and end apart: 6, of which 4 were waited for; matrix products, arithmetic and copies ran while one was open for 12% of the time, Pallas kernels for 0%

commit v1 on v0

--- a/solution.py
+++ b/solution.py
@@ -97,7 +97,7 @@
         TAPS, channels, own_width
     )
     stacked = jnp.stack([first_grad, second_grad])
-    summed = lax.psum(stacked, ("replica", "tm"))
+    summed = lax.psum(lax.psum(stacked, "tm"), "replica")
     tap_mixed = jnp.einsum("lst,ltij->lsij", tap_mix, summed, precision=highest)
     left_done = jnp.einsum(
         "lik,lskj->lsij",

time: 500 us -> 623 us (1.25)
  the two profiles are of different devices: /device:TPU:4 before, /device:TPU:2 now
where the time goes in v1:
time: 623 us; the launch traced here: 613 us
  waiting for transfers between devices  347 us (56%)
  local copies, waits for them, and re-layouts  166 us (27%)
  other arithmetic  45.9 us (7%)
  matrix products  30.9 us (5%)
  between operations  16 us (3%)
  starting transfers between devices  7.29 us (1%)
    psum x2, waiting for transfers between devices, shards(): summed = lax.psum(lax.psum(stacked, 'tm'), 'replica')  266 us
    slice x54, local copies, waits for them, and re-layouts, tap_patches(): padded[:, along_time:along_time + 2 * out_frames:2, along_rows:along_rows...  120 us
    unnamed x5, waiting for transfers between devices  75.6 us
    scatter-add x27, other arithmetic, spread_back(): total = total.at[:, along_time:along_time + 2 * out_frames:2, along_rows:...  40.8 us
    unnamed x58, local copies, waits for them, and re-layouts  33.9 us
  transfers between devices with their start and end apart: 7, of which 4 were waited for; matrix products, arithmetic and copies ran while one was open for 10% of the time, Pallas kernels for 0%

profile of v1, /device:TPU:2, one launch (start us, length us, event | category | flops | bytes accessed | tf_op | source)
XLA Modules:
  0.0 613.0 jit_solution(5589824426056030264)
XLA Ops:
  8.5 4.0 collective-permute-start
  60.4 5.0 collective-permute-done.1
  67.9 5.0 slice.318
  72.9 4.9 slice.319
  77.8 5.0 slice.320
  82.8 4.9 slice.321
  87.7 4.9 slice.322
  92.7 5.0 slice.323
  97.6 5.0 slice.324
  102.6 4.9 slice.325
  107.5 5.0 slice.326
  112.5 4.9 slice.327
  117.4 4.9 slice.328
  122.4 5.0 slice.329
  127.3 4.9 slice.330
  132.2 4.9 slice.331
  137.2 5.0 slice.332
  142.1 4.9 slice.333
  147.1 4.9 slice.334
  152.0 5.0 slice.335
  157.0 4.9 slice.336
  161.9 4.9 slice.337
  166.8 5.0 slice.338
  171.8 4.9 slice.339
  176.7 4.9 slice.340
  215.6 6.0 copy.17
  226.6 3.3 convolution_bitcast_fusion
  237.0 121.3 %all-reduce.5.cloned.1.call-done = f32[2,27,512,32]{2,3,1,0:T(8,128)} async-done(((f32[2,27,512,32]{2,3,1,0:T(8,128)}), f32[2,27,512,32]{2,3,1,0:T(8,128)}) %all-reduce.5.cloned.1.call-update) | async-done | bytes 3538960 | tf_op jit(solution)/shard_map/psum | solution.py:100
  359.2 144.8 %all-reduce.7.cloned.1.call-done = f32[2,27,512,32]{2,3,1,0:T(8,128)} async-done(((f32[2,27,512,32]{2,3,1,0:T(8,128)}), f32[2,27,512,32]{2,3,1,0:T(8,128)}) %all-reduce.7.cloned.1.call-update) | async-done | bytes 3538960 | tf_op jit(solution)/shard_map/psum | solution.py:100
  504.0 10.7 %fusion.11 = f32[2,27,512,32]{2,1,3,0:T(8,128)} fusion(f32[2,27,512,32]{2,3,1,0:T(8,128)} %all-reduce.7.cloned.1.call-done, f32[2,27,27,1]{2,0,1,3:T(2,128)S(1)} %bitcast.215), kind=kOutput, calls=%fused_computation.41 | convolution fusion | flops 286654464 | bytes 7083720 | tf_op jit(solution)/shard_map/lst,ltij->lsij/dot_general | solution.py:101
  514.7 10.1 %fusion.7 = f32[2,27,32,512]{3,2,1,0:T(8,128)S(1)} fusion(f32[2,27,512,32]{2,1,3,0:T(8,128)} %fusion.11, f32[2,512,512]{2,1,0:T(8,128)} %all-gather.2.cloned.1.call-done), kind=kOutput, calls=%fused_computation.37 | convolution fusion | flops 5435817984 | bytes 9175040 | tf_op jit(solution)/shard_map/lik,lskj->lsij/dot_general | solution.py:102
  528.6 75.0 %reduce-scatter.4.cloned.1.call-done = f32[32,864]{1,0:T(8,128)} async-done(((f32[512,864]{1,0:T(8,128)}), f32[32,864]{1,0:T(8,128)}) %reduce-scatter.4.cloned.1.call-update) | async-done | bytes 110608
  (209 shorter events, 102.9 us)
Async XLA Ops:
  7.4 5.8 copy-start
  7.4 52.1 %copy-start.2 = (bf16[27,512,32]{1,2,0:T(8,128)(2,1)S(1)}, bf16[27,512,32]{1,2,0:T(8,128)(2,1)}, u32[]{:S(2)}) copy-start(bf16[27,512,32]{1,2,0:T(8,128)(2,1)} %param.10) | copy-start | bytes 2654212
  7.4 350.9 %all-reduce.5.cloned.1.call-start = ((), (), s32[]{:S(2)}) async-start(), calls=%async_computation.1 | async-start | bytes 7077888 | tf_op jit(solution)/shard_map/psum | solution.py:100
  8.5 57.3 %collective-permute-start = (bf16[1,1,16,16,512]{4,3,2,1,0:T(8,128)(2,1)S(1)}, bf16[1,1,16,16,512]{4,3,2,1,0:T(8,128)(2,1)S(1)}, u32[]{:S(2)}, u32[]{:S(2)}) collective-permute-start(bf16[1,1,16,16,512]{4,3,2,1,0:T(8,128)(2,1)S(1)} %slice.317), channel_id=1, source_target_pairs={{0,1},{2,3},{4,5},{6,7},{8,9},{10,11},{12,13},{14,15},{16,17},{18,... | collective-permute-start | bytes 786440 | tf_op jit(solution)/shard_map/ppermute | solution.py:12
  58.1 7.3 %collective-permute-start.1 = (f32[1,1,8,8,32]{4,1,3,2,0:T(1,128)S(1)}, f32[1,1,8,8,32]{4,1,3,2,0:T(1,128)S(1)}, u32[]{:S(2)}, u32[]{:S(2)}) collective-permute-start(f32[1,1,8,8,32]{4,1,3,2,0:T(1,128)S(1)} %slice.702), channel_id=1, source_target_pairs={{1,0},{3,2},{5,4},{7,6},{9,8},{11,10},{13,12},{15,14},{17,16},{19,... | collective-permute-start | bytes 24584 | tf_op jit(solution)/shard_map/ppermute | solution.py:12
  184.4 22.4 %copy-start.11 = (bf16[1,2,8,8,512]{4,3,2,1,0:T(8,128)(2,1)S(1)}, bf16[1,2,8,8,512]{4,3,2,1,0:T(8,128)(2,1)}, u32[]{:S(2)}) copy-start(bf16[1,2,8,8,512]{4,3,2,1,0:T(8,128)(2,1)} %slice.332) | copy-start | bytes 393220
  184.4 23.1 %copy-start.10 = (bf16[1,2,8,8,512]{4,3,2,1,0:T(8,128)(2,1)S(1)}, bf16[1,2,8,8,512]{4,3,2,1,0:T(8,128)(2,1)}, u32[]{:S(2)}) copy-start(bf16[1,2,8,8,512]{4,3,2,1,0:T(8,128)(2,1)} %slice.333) | copy-start | bytes 393220
  184.4 23.7 %copy-start.9 = (bf16[1,2,8,8,512]{4,3,2,1,0:T(8,128)(2,1)S(1)}, bf16[1,2,8,8,512]{4,3,2,1,0:T(8,128)(2,1)}, u32[]{:S(2)}) copy-start(bf16[1,2,8,8,512]{4,3,2,1,0:T(8,128)(2,1)} %slice.334) | copy-start | bytes 393220
  184.4 24.4 %copy-start.8 = (bf16[1,2,8,8,512]{4,3,2,1,0:T(8,128)(2,1)S(1)}, bf16[1,2,8,8,512]{4,3,2,1,0:T(8,128)(2,1)}, u32[]{:S(2)}) copy-start(bf16[1,2,8,8,512]{4,3,2,1,0:T(8,128)(2,1)} %slice.335) | copy-start | bytes 393220
  184.4 25.1 %copy-start.7 = (bf16[1,2,8,8,512]{4,3,2,1,0:T(8,128)(2,1)S(1)}, bf16[1,2,8,8,512]{4,3,2,1,0:T(8,128)(2,1)}, u32[]{:S(2)}) copy-start(bf16[1,2,8,8,512]{4,3,2,1,0:T(8,128)(2,1)} %slice.336) | copy-start | bytes 393220
  184.4 25.8 %copy-start.6 = (bf16[1,2,8,8,512]{4,3,2,1,0:T(8,128)(2,1)S(1)}, bf16[1,2,8,8,512]{4,3,2,1,0:T(8,128)(2,1)}, u32[]{:S(2)}) copy-start(bf16[1,2,8,8,512]{4,3,2,1,0:T(8,128)(2,1)} %slice.337) | copy-start | bytes 393220
  184.4 26.4 %copy-start.5 = (bf16[1,2,8,8,512]{4,3,2,1,0:T(8,128)(2,1)S(1)}, bf16[1,2,8,8,512]{4,3,2,1,0:T(8,128)(2,1)}, u32[]{:S(2)}) copy-start(bf16[1,2,8,8,512]{4,3,2,1,0:T(8,128)(2,1)} %slice.338) | copy-start | bytes 393220
  184.4 27.1 %copy-start.4 = (bf16[1,2,8,8,512]{4,3,2,1,0:T(8,128)(2,1)S(1)}, bf16[1,2,8,8,512]{4,3,2,1,0:T(8,128)(2,1)}, u32[]{:S(2)}) copy-start(bf16[1,2,8,8,512]{4,3,2,1,0:T(8,128)(2,1)} %slice.339) | copy-start | bytes 393220
  184.5 27.7 %copy-start.3 = (bf16[1,2,8,8,512]{4,3,2,1,0:T(8,128)(2,1)S(1)}, bf16[1,2,8,8,512]{4,3,2,1,0:T(8,128)(2,1)}, u32[]{:S(2)}) copy-start(bf16[1,2,8,8,512]{4,3,2,1,0:T(8,128)(2,1)} %slice.340) | copy-start | bytes 393220
  215.6 6.0 copy-start.1
  224.8 9.4 %copy-start.14 = (bf16[1,1,4,4,512]{4,3,2,1,0:T(4,128)(2,1)S(1)}, bf16[1,1,4,4,512]{4,3,2,1,0:T(4,128)(2,1)}, u32[]{:S(2)}) copy-start(bf16[1,1,4,4,512]{4,3,2,1,0:T(4,128)(2,1)} %param.12) | copy-start | bytes 49156
  225.0 4.9 collective-permute-start.2
  236.9 267.1 %copy-start.12 = (f32[2,27,27]{2,0,1:T(2,128)S(1)}, f32[2,27,27]{2,0,1:T(2,128)}, u32[]{:S(2)}) copy-start(f32[2,27,27]{2,0,1:T(2,128)} %param.13) | copy-start | bytes 17500
  236.9 267.1 %all-reduce.7.cloned.1.call-start = ((), (), s32[]{:S(2)}) async-start(), calls=%async_computation.2 | async-start | bytes 7077888 | tf_op jit(solution)/shard_map/psum | solution.py:100
  358.3 156.4 %all-gather.2.cloned.1.call-start = ((), (), s32[]{:S(2)}) async-start(), calls=%async_computation.3 | async-start | bytes 2228224 | tf_op jit(solution)/shard_map/all_gather | solution.py:104
  358.9 244.7 %reduce-scatter.4.cloned.1.call-start = ((), (), s32[]{:S(2)}) async-start(), calls=%async_computation.4 | async-start | bytes 1949696
  514.7 10.1 %copy-start.13 = (f32[2,32,16]{1,2,0:T(8,128)S(1)}, f32[2,32,16]{1,2,0:T(8,128)}, u32[]{:S(2)}) copy-start(f32[2,32,16]{1,2,0:T(8,128)} %param.15) | copy-start | bytes 12292
Sparse Core Ops, SparseCore 0:
  237.0 121.2 all-reduce.4
  361.3 142.6 all-reduce.6
Sparse Core Ops, SparseCore 1:
  360.9 73.3 all-gather.1
  528.7 74.9 reduce-scatter.3
